TPU v7x, 128 devices: a whole 4x4x4 slice. The times are simulated.
128 devices in a mesh: ctx: 32 (over z, x, core), exp: 4 (over y).
Axes of the slice: x: 4, y: 4, z: 4, core: 2. Of those that a mesh axis runs over, the one named last changes fastest.
Arguments:
- queries: bfloat16 [8192, 4096], P('ctx', 'exp'), may hold values from -6 to 6
- key_rows: bfloat16 [8192, 4096], P('ctx', 'exp'), may hold values from -6 to 6
- value_rows: bfloat16 [8192, 4096], P('ctx', 'exp'), may hold values from -6 to 6
- gate_rows: bfloat16 [8192, 4096], P('ctx', 'exp'), may hold values from -6 to 6
- decay_exp: int32 [32], P('exp'), may hold values from 5 to 16
- attn_gain: float32 [4096], P('exp'), may hold values from 0.1 to 1.9
- out_proj: bfloat16 [4096, 6144], P('exp'), may hold values from -0.09375 to 0.09375
- residual: bfloat16 [8192, 6144], P(('ctx', 'exp')), may hold values from -6 to 6
- norm_gain: float32 [6144], replicated, may hold values from 0.1 to 1.9
- routes: int32 [8192, 2], P('ctx'), may hold values from 0 to 31, as said below
- route_weights: float32 [8192, 2], P('ctx'), may hold values from 0.1 to 1
- w_gate: bfloat16 [4, 9216, 6144], P('exp', 'ctx'), may hold values from -0.078125 to 0.078125
- w_up: bfloat16 [4, 9216, 6144], P('exp', 'ctx'), may hold values from -0.078125 to 0.078125
- w_down: bfloat16 [4, 9216, 6144], P('exp', 'ctx'), may hold values from -0.0625 to 0.0625
Outputs:
- layer_out: bfloat16 [8192, 6144], P(('ctx', 'exp'))
Inputs may be any that keep to these rules, and one draw needn't show every extreme that they name: `routes`: A row's two entries differ. An expert e below 4 is named only in column e % 2. In every aligned block of 64 rows each expert below 4 is named at most 8 times, and some expert below 4 exactly 8 times.
All inputs are finite; a program needn't handle non-finite values.
Results may differ from a plain program's by a relative error of at most 0.018.
Values may be sent and summed in bfloat16 or wider, within the bound.
A program may use at most 128 MiB of HBM per device.

v0:
```python
import jax
import jax.numpy as jnp
from jax import lax
from jax.sharding import PartitionSpec as P

EPSILON = 1e-06


def earlier_states(update, decay_rates, row_count):
    size, index = (lax.axis_size("ctx"), lax.axis_index("ctx"))
    everything = lax.all_gather(update.astype(jnp.bfloat16), "ctx").astype(jnp.float32)
    distance = (index - 1 - jnp.arange(size)).astype(jnp.float32)
    factors = jnp.where(
        distance[:, None] >= 0.0,
        jnp.exp(-decay_rates[None, :] * row_count * jnp.maximum(distance, 0.0)[:, None]),
        0.0,
    )
    return jnp.sum(everything * factors[:, :, None, None], axis=0)


def span_local(queries, key_rows, value_rows, decay_exp):
    row_count = queries.shape[0]
    head_count = decay_exp.shape[0]
    head_width = queries.shape[1] // head_count
    query_heads = queries.reshape(row_count, head_count, head_width)
    key_heads = key_rows.reshape(row_count, head_count, head_width)
    value_heads = value_rows.reshape(row_count, head_count, head_width)
    decay_rates = jnp.exp2(-decay_exp.astype(jnp.float32))
    positions = jnp.arange(row_count, dtype=jnp.float32)
    offsets = positions[:, None] - positions[None, :]
    damping = jnp.where(
        offsets[None] >= 0.0,
        jnp.exp(-decay_rates[:, None, None] * jnp.maximum(offsets, 0.0)[None]),
        0.0,
    )
    scores = jnp.einsum("thd,shd->hts", query_heads, key_heads, preferred_element_type=jnp.float32)
    mixing = (scores * damping).astype(jnp.bfloat16)
    inner_part = jnp.einsum("hts,shd->thd", mixing, value_heads, preferred_element_type=jnp.float32)
    tail_decay = jnp.exp(-decay_rates[None, :] * (row_count - 1.0 - positions)[:, None])
    keyed_rows = (key_heads.astype(jnp.float32) * tail_decay[:, :, None]).astype(jnp.bfloat16)
    update = jnp.einsum("shd,she->hde", keyed_rows, value_heads, preferred_element_type=jnp.float32)
    lead_decay = jnp.exp(-decay_rates[None, :] * (positions + 1.0)[:, None])
    leading = query_heads.astype(jnp.float32) * lead_decay[:, :, None]
    return (inner_part, leading, update, decay_rates)


def settle(inner_part, leading, prior_state, gate_rows, attn_gain):
    outer_part = jnp.einsum("thd,hde->the", leading, prior_state, precision=lax.Precision.HIGHEST)
    mixed_heads = inner_part + outer_part
    row_count, head_count, head_width = mixed_heads.shape
    mean_square = jnp.mean(mixed_heads * mixed_heads, axis=2, keepdims=True)
    normed_heads = mixed_heads * lax.rsqrt(mean_square + EPSILON)
    gain_heads = attn_gain.reshape(head_count, head_width)
    gate_heads = gate_rows.reshape(row_count, head_count, head_width).astype(jnp.float32)
    settled = (normed_heads * gain_heads * jax.nn.sigmoid(gate_heads)).astype(jnp.bfloat16)
    return settled.reshape(row_count, head_count * head_width)


def token_norm(hidden, norm_gain):
    mean_square = jnp.mean(hidden * hidden, axis=1, keepdims=True)
    return (hidden * lax.rsqrt(mean_square + EPSILON) * norm_gain).astype(jnp.bfloat16)


def slot_table(chosen_ids, expert_count, capacity):
    owners = jnp.arange(expert_count, dtype=jnp.int32)
    chosen = jnp.where(owners[:, None] % 2 == 0, chosen_ids[None, :, 0], chosen_ids[None, :, 1])
    picked = chosen == owners[:, None]
    row_count = chosen_ids.shape[0]
    upto = jnp.arange(row_count)[:, None] <= jnp.arange(row_count)[None, :]
    slot_rank = jnp.dot(picked.astype(jnp.float32), upto.astype(jnp.float32)) - 1.0
    slot_ids = jnp.arange(capacity, dtype=jnp.float32)
    return picked[:, None, :] & (slot_rank[:, None, :] == slot_ids[None, :, None])


def expert_part(slot_rows, gate_cols, up_cols, down_rows):
    contract_dims = (((1,), (1,)), ((), ()))
    first_half = lax.dot_general(
        slot_rows, gate_cols, contract_dims, preferred_element_type=jnp.float32
    )
    second_half = lax.dot_general(
        slot_rows, up_cols, contract_dims, preferred_element_type=jnp.float32
    )
    activated = (jax.nn.silu(first_half) * second_half).astype(jnp.bfloat16)
    return jnp.dot(activated, down_rows, preferred_element_type=jnp.float32)


def body(
    queries,
    key_rows,
    value_rows,
    gate_rows,
    decay_exp,
    attn_gain,
    out_proj,
    residual,
    norm_gain,
    routes,
    route_weights,
    w_gate,
    w_up,
    w_down,
):
    inner_part, leading, update, decay_rates = span_local(queries, key_rows, value_rows, decay_exp)
    span_rows = queries.shape[0]
    prior_state = earlier_states(update, decay_rates, span_rows)
    settled = settle(inner_part, leading, prior_state, gate_rows, attn_gain)
    group_count = lax.axis_size("exp")
    group_rows = span_rows // group_count
    first_mine = lax.axis_index("exp") * group_rows
    capacity = group_rows // 8
    projected = jnp.dot(settled, out_proj, preferred_element_type=jnp.float32)
    summed = lax.psum_scatter(
        projected.astype(jnp.bfloat16), "exp", scatter_dimension=0, tiled=True
    ).astype(jnp.float32)
    hidden = summed + residual.astype(jnp.float32)
    normed = token_norm(hidden, norm_gain)
    my_routes = lax.dynamic_slice_in_dim(routes, first_mine, group_rows, 0)
    my_weights = lax.dynamic_slice_in_dim(route_weights, first_mine, group_rows, 0)
    table = slot_table(my_routes, group_count, capacity)
    outgoing = jnp.einsum(
        "ecn,nd->ecd", table.astype(jnp.bfloat16), normed, preferred_element_type=jnp.float32
    ).astype(jnp.bfloat16)
    mine = lax.all_to_all(outgoing, "exp", 0, 0, tiled=True)
    mine = mine.reshape(group_count * capacity, -1)
    gathered = lax.all_gather(mine, "ctx", axis=0, tiled=True)
    produced = lax.psum_scatter(
        expert_part(gathered, w_gate[0], w_up[0], w_down[0]).astype(jnp.bfloat16),
        "ctx",
        scatter_dimension=0,
        tiled=True,
    )
    produced = produced.reshape(group_count, capacity, -1)
    returned = lax.all_to_all(produced, "exp", 0, 0, tiled=True)
    for column in range(2):
        fetched = jnp.einsum(
            "ecn,ecd->nd",
            table[column::2].astype(jnp.bfloat16),
            returned[column::2],
            preferred_element_type=jnp.float32,
        )
        hidden = hidden + my_weights[:, column][:, None] * fetched
    return hidden.astype(jnp.bfloat16)


def solution(mesh):
    in_specs = (
        P("ctx", "exp"),
        P("ctx", "exp"),
        P("ctx", "exp"),
        P("ctx", "exp"),
        P("exp"),
        P("exp"),
        P("exp", None),
        P(("ctx", "exp"), None),
        P(),
        P("ctx", None),
        P("ctx", None),
        P("exp", "ctx", None),
        P("exp", "ctx", None),
        P("exp", "ctx", None),
    )
    out_specs = P(("ctx", "exp"), None)
    return jax.shard_map(body, mesh=mesh, in_specs=in_specs, out_specs=out_specs, check_vma=False)
```

profile of v0, /device:TPU:0, one launch (start us, length us, event | category | flops | bytes accessed | tf_op | source)
XLA Modules:
  0.0 362.1 jit_solution(7711785279852202598)
XLA Ops:
  6.5 0.0 copy-start
  6.5 0.0 all-gather.6.cloned.1.call-start
  6.5 1.4 broadcast_multiply_fusion
  7.9 2.0 copy.27
  10.0 0.7 multiply_exponential_fusion
  10.7 2.2 convolution_convert_fusion.3
  12.9 0.0 all-gather.6.cloned.1.call-update
  12.9 0.0 reduce-scatter.3.cloned.1.call-start
  13.0 2.3 add_divide_fusion
  15.2 0.0 copy-done.6
  15.2 2.6 copy.25
  17.9 0.7 fusion.46
  18.6 0.8 fusion.45
  19.4 0.7 exponential_select_fusion
  20.1 48.4 %all-gather.6.cloned.1.call-done = bf16[256,128,128]{2,1,0:T(8,128)(2,1)} async-done(((bf16[8,128,128]{2,1,0:T(8,128)(2,1)}), bf16[256,128,128]{2,1,0:T(8,128)(2,1)}) %all-gather.6.cloned.1.call-update) | async-done | bytes 8388624 | tf_op jit(solution)/shard_map/all_gather | solution.py:11
  68.5 5.2 %fusion = f32[8,128,128]{2,1,0:T(8,128)S(1)} fusion(bf16[32,8,128,128]{3,2,1,0:T(8,128)(2,1)} %bitcast.93, f32[32,8]{1,0:T(8,128)S(1)} %exponential_select_fusion), kind=kLoop, calls=%fused_computation.1 | loop fusion | flops 12451840 | bytes 8913920 | tf_op jit(solution)/shard_map/reduce_sum | solution.py:18
  73.7 0.0 copy-start.7
  73.7 0.0 copy-done.3
  73.7 0.0 copy-done.4
  73.7 2.4 convolution_bitcast_fusion.2
  76.1 3.7 %multiply_reduce_fusion.1 = (f32[256,8]{0,1:T(8,128)S(1)}, f32[256,8,128]{0,2,1:T(8,128)}) fusion(f32[256,8,128]{0,2,1:T(8,128)} %convolution_bitcast_fusion.2, bf16[256,8,128]{0,2,1:T(8,128)(2,1)} %bitcast.98, f32[256,256]{1,0:T(8,128)} %fusion.45, f32[8]{0:T(128)S(1)} %copy-done.7, pred[256,256]{1,0:T(8,128)(4,1)} %fusion.46, ...), kind=kOutput, calls=%fused_computation.31 | convolution fusion | flops 271316992 | bytes 4005920 | tf_op jit(solution)/shard_map/hts,shd->thd/dot_general | solution.py:38
  79.8 1.8 multiply_convert_fusion.2
  81.6 9.5 %convolution_convert_fusion.1 = bf16[256,6144]{1,0:T(8,128)(2,1)} fusion(bf16[256,1024]{0,1:T(8,128)(2,1)S(1)} %bitcast.95, bf16[1024,6144]{1,0:T(8,128)(2,1)} %param.20), kind=kOutput, calls=%fused_computation.3 | convolution fusion | flops 3222798336 | bytes 16252928 | tf_op jit(solution)/shard_map/dot_general | solution.py:111
  91.1 0.0 reduce-scatter.3.cloned.1.call-update
  91.1 0.0 all-gather.4.cloned.1.call-start
  91.2 0.6 copy-done.8
  91.8 0.1 constant_dynamic-slice_fusion
  91.9 0.1 iota_compare_fusion.3
  91.9 0.1 convolution_add_fusion
  92.1 37.0 %reduce-scatter.3.cloned.1.call-done = bf16[64,6144]{1,0:T(8,128)(2,1)} async-done(((bf16[256,6144]{1,0:T(8,128)(2,1)}), bf16[64,6144]{1,0:T(8,128)(2,1)}) %reduce-scatter.3.cloned.1.call-update) | async-done | bytes 786448 | tf_op jit(solution)/shard_map/reduce_scatter | solution.py:112
  129.1 1.7 multiply_reduce_fusion
  130.9 1.8 convolution_convert_fusion.2
  132.7 11.5 %all_to_all.10 = bf16[4,8,6144]{2,1,0:T(8,128)(2,1)} all-to-all(bf16[4,8,6144]{2,1,0:T(8,128)(2,1)S(1)} %convolution_convert_fusion.2), channel_id=1, replica_groups=mesh['ctx'=32,'exp'=4] {'exp'}, dimensions={0} | all-to-all | bytes 786432 | tf_op jit(solution)/shard_map/all_to_all | solution.py:123
  144.2 0.0 all-gather.4.cloned.1.call-update
  144.2 0.2 reduce-scatter.5.cloned.1.call-start
  144.4 62.3 %all-gather.4.cloned.1.call-done = bf16[1024,6144]{1,0:T(8,128)(2,1)} async-done(((bf16[32,6144]{1,0:T(8,128)(2,1)}), bf16[1024,6144]{1,0:T(8,128)(2,1)}) %all-gather.4.cloned.1.call-update) | async-done | bytes 12582928 | tf_op jit(solution)/shard_map/all_gather | solution.py:125
  206.7 10.5 %fusion.9 = f32[1024,288]{0,1:T(8,128)} fusion(bf16[1024,6144]{1,0:T(8,128)(2,1)} %all-gather.4.cloned.1.call-done, bf16[1,288,6144]{2,1,0:T(8,128)(2,1)} %param.25), kind=kOutput, calls=%fused_computation.15 | convolution fusion | flops 3623878656 | bytes 17301504 | tf_op jit(solution)/shard_map/dot_general | solution.py:77
  217.2 17.6 %convolution_convert_fusion = bf16[1024,6144]{1,0:T(8,128)(2,1)} fusion(bf16[1,288,6144]{2,1,0:T(8,128)(2,1)S(1)} %copy-done, bf16[1024,6144]{1,0:T(8,128)(2,1)} %all-gather.4.cloned.1.call-done, bf16[1,288,6144]{2,1,0:T(8,128)(2,1)} %param.26, f32[1024,288]{0,1:T(8,128)} %fusion.9), kind=kOutput, calls=%fused_computation.2 | convolution fusion | flops 7255818240 | bytes 33423360 | tf_op jit(solution)/shard_map/dot_general | solution.py:84
  234.8 0.0 reduce-scatter.5.cloned.1.call-update
  234.9 0.7 copy-done.9
  235.5 0.1 constant_dynamic-slice_fusion.1
  235.6 103.3 %reduce-scatter.5.cloned.1.call-done = bf16[32,6144]{1,0:T(8,128)(2,1)} async-done(((bf16[1024,6144]{1,0:T(8,128)(2,1)}), bf16[32,6144]{1,0:T(8,128)(2,1)}) %reduce-scatter.5.cloned.1.call-update) | async-done | bytes 393232 | tf_op jit(solution)/shard_map/reduce_scatter | solution.py:126
  338.9 4.3 %all-to-all-start.1 = ((bf16[4,8,6144]{2,1,0:T(8,128)(2,1)}), bf16[4,8,6144]{2,1,0:T(8,128)(2,1)S(1)}, u32[]{:S(2)}, u32[]{:S(2)}) async-start(bf16[4,8,6144]{2,1,0:T(8,128)(2,1)} %bitcast.99), calls=%async_computation.3 | async-start | bytes 786432 | tf_op jit(solution)/shard_map/all_to_all | solution.py:133
  343.1 0.5 slice_bitcast_fusion.3
  343.7 6.9 %all-to-all-done.1 = bf16[4,8,6144]{2,1,0:T(8,128)(2,1)S(1)} async-done(((bf16[4,8,6144]{2,1,0:T(8,128)(2,1)}), bf16[4,8,6144]{2,1,0:T(8,128)(2,1)S(1)}, u32[]{:S(2)}, u32[]{:S(2)}) %all-to-all-start.1) | async-done | bytes 393248 | tf_op jit(solution)/shard_map/all_to_all | solution.py:133
  350.5 0.7 copy-done.2
  351.3 1.5 fusion.4
  352.8 2.8 fusion.5
  (20 shorter events, 0.1 us)
Async XLA Ops:
  6.5 210.7 %copy-start = (bf16[1,288,6144]{2,1,0:T(8,128)(2,1)S(1)}, bf16[1,288,6144]{2,1,0:T(8,128)(2,1)}, u32[]{:S(2)}) copy-start(bf16[1,288,6144]{2,1,0:T(8,128)(2,1)} %param.27) | copy-start | bytes 10616836
  6.5 62.0 %all-gather.6.cloned.1.call-start = ((), (), s32[]{:S(2)}) async-start(), calls=%async_computation.7 | async-start | bytes 8650752 | tf_op jit(solution)/shard_map/all_gather | solution.py:11
  7.9 7.3 %copy-start.6 = (f32[8]{0:T(128)}, f32[8]{0:T(128)S(1)}, u32[]{:S(2)}) copy-start(f32[8]{0:T(128)S(1)} %get-tuple-element.6) | copy-start | bytes 100
  12.9 116.2 %reduce-scatter.3.cloned.1.call-start = ((), (), s32[]{:S(2)}) async-start(), calls=%async_computation.4 | async-start | bytes 3932160 | tf_op jit(solution)/shard_map/reduce_scatter | solution.py:112
  68.5 5.2 %copy-start.3 = (bf16[256,1024]{1,0:T(8,128)(2,1)S(1)}, bf16[256,1024]{1,0:T(8,128)(2,1)}, u32[]{:S(2)}) copy-start(bf16[256,1024]{1,0:T(8,128)(2,1)} %param.14) | copy-start | bytes 1572868
  68.5 5.2 %copy-start.4 = (f32[256,8]{0,1:T(8,128)S(1)}, f32[256,8]{0,1:T(8,128)}, u32[]{:S(2)}) copy-start(f32[256,8]{0,1:T(8,128)} %get-tuple-element.11) | copy-start | bytes 24580
  73.7 2.4 copy-start.7
  76.1 3.7 %copy-start.5 = (f32[1024]{0:T(1024)S(1)}, f32[1024]{0:T(1024)}, u32[]{:S(2)}) copy-start(f32[1024]{0:T(1024)} %param.19) | copy-start | bytes 12292
  91.1 0.7 copy-start.8
  91.1 115.6 %all-gather.4.cloned.1.call-start = ((), (), s32[]{:S(2)}) async-start(), calls=%async_computation.5 | async-start | bytes 12976128 | tf_op jit(solution)/shard_map/all_gather | solution.py:125
  144.2 194.7 %reduce-scatter.5.cloned.1.call-start = ((), (), s32[]{:S(2)}) async-start(), calls=%async_computation.6 | async-start | bytes 12976128 | tf_op jit(solution)/shard_map/reduce_scatter | solution.py:126
  234.8 0.7 copy-start.9
  338.9 11.7 %all-to-all-start.1 = ((bf16[4,8,6144]{2,1,0:T(8,128)(2,1)}), bf16[4,8,6144]{2,1,0:T(8,128)(2,1)S(1)}, u32[]{:S(2)}, u32[]{:S(2)}) async-start(bf16[4,8,6144]{2,1,0:T(8,128)(2,1)} %bitcast.99), calls=%async_computation.3 | async-start | bytes 786432 | tf_op jit(solution)/shard_map/all_to_all | solution.py:133
  350.5 0.7 copy-start.2
  351.3 4.3 %copy-start.1 = (bf16[1,288,6144]{2,1,0:T(8,128)(2,1)S(1)}, bf16[1,288,6144]{2,1,0:T(8,128)(2,1)}, u32[]{:S(2)}) copy-start(bf16[1,288,6144]{2,1,0:T(8,128)(2,1)} %param.27) | copy-start | bytes 10616836
Sparse Core Ops, SparseCore 0:
  13.0 55.4 all-gather.5
  91.2 37.8 reduce-scatter.2
  144.3 62.3 all-gather.3
  235.0 103.8 reduce-scatter.4
where the time goes:
time: 363 us; the launch traced here: 362 us
  waiting for transfers between devices  258 us (71%)
  matrix products  52.1 us (14%)
  other arithmetic  15.3 us (4%)
  between operations  13.2 us (4%)
  blocking collectives  11.5 us (3%)
  local copies, waits for them, and re-layouts  7.34 us (2%)
  starting transfers between devices  4.58 us (1%)
    reduce_scatter x1, waiting for transfers between devices, body(): lax.psum_scatter(expert_part(gathered, w_gate[0], w_up[0], w_down[0]).ast...  103 us
    all_gather x1, waiting for transfers between devices, body(): gathered = lax.all_gather(mine, 'ctx', axis=0, tiled=True)  62.3 us
    all_gather x1, waiting for transfers between devices, earlier_states(): lax.all_gather(update.astype(jnp.bfloat16), 'ctx').astype(jnp.float32)  48.4 us
    reduce_scatter x1, waiting for transfers between devices, body(): lax.psum_scatter(projected.astype(jnp.bfloat16), 'exp', scatter_dimension...  37 us
    dot_general x1, matrix products, expert_part(): return jnp.dot(activated, down_rows, preferred_element_type=jnp.float32)  17.6 us
    all_to_all x1, blocking collectives, body(): mine = lax.all_to_all(outgoing, 'exp', 0, 0, tiled=True)  11.5 us
    dot_general x1, matrix products, expert_part(): lax.dot_general(slot_rows, gate_cols, contract_dims, preferred_element_ty...  10.5 us
    dot_general x1, matrix products, body(): projected = jnp.dot(settled, out_proj, preferred_element_type=jnp.float32)  9.51 us
  transfers between devices with their start and end apart: 5, of which 5 were waited for; matrix products, arithmetic and copies ran while one was open for 2% of the time, Pallas kernels for 0%

commit v1 on v0

--- a/solution.py
+++ b/solution.py
@@ -122,7 +122,10 @@
     ).astype(jnp.bfloat16)
     mine = lax.all_to_all(outgoing, "exp", 0, 0, tiled=True)
     mine = mine.reshape(group_count * capacity, -1)
-    gathered = lax.all_gather(mine, "ctx", axis=0, tiled=True)
+    count = lax.axis_size("ctx")
+    blocks = jnp.stack([mine for _ in range(count)])
+    blocks = lax.all_to_all(blocks, "ctx", split_axis=0, concat_axis=0)
+    gathered = jnp.concatenate(blocks, axis=0)
     produced = lax.psum_scatter(
         expert_part(gathered, w_gate[0], w_up[0], w_down[0]).astype(jnp.bfloat16),
         "ctx",

time: 363 us -> 451 us (1.24)
  blocking collectives: 11.5 us -> 159 us
  waiting for transfers between devices: 258 us -> 195 us
  local copies, waits for them, and re-layouts: 7.34 us -> 17.2 us
  matrix products: 52.1 us -> 46.1 us
    all_to_all x0 -> x1, blocking collectives: none -> 148 us  [body(): blocks = lax.all_to_all(blocks, 'ctx', split_axis=0, concat_axis=0)]
    all_gather x1 -> x0, waiting for transfers between devices: 62.3 us -> none  [body(): gathered = lax.all_gather(mine, 'ctx', axis=0, tiled=True)]
    another operation x0 -> x1, local copies, waits for them, and re-layouts: none -> 6.1 us  [body(): blocks = jnp.stack([mine for _ in range(count)])]
    dot_general x1, matrix products: 10.5 us -> 4.99 us  [expert_part(): lax.dot_general(slot_rows, gate_cols, contract_dims, preferred_element_ty...]
  transfers between devices with their start and end apart: 5 -> 4, of which waited for: 5 -> 4; matrix products, arithmetic and copies ran while one was open for 2% -> 2% of each run, Pallas kernels for 0% -> 0%
where the time goes in v1:
time: 451 us; the launch traced here: 450 us
  waiting for transfers between devices  195 us (43%)
  blocking collectives  159 us (35%)
  matrix products  46.1 us (10%)
  local copies, waits for them, and re-layouts  17.2 us (4%)
  other arithmetic  15.2 us (3%)
  between operations  13.2 us (3%)
    all_to_all x1, blocking collectives, body(): blocks = lax.all_to_all(blocks, 'ctx', split_axis=0, concat_axis=0)  148 us
    reduce_scatter x1, waiting for transfers between devices, body(): lax.psum_scatter(expert_part(gathered, w_gate[0], w_up[0], w_down[0]).ast...  102 us
    all_gather x1, waiting for transfers between devices, earlier_states(): lax.all_gather(update.astype(jnp.bfloat16), 'ctx').astype(jnp.float32)  48.5 us
    reduce_scatter x1, waiting for transfers between devices, body(): lax.psum_scatter(projected.astype(jnp.bfloat16), 'exp', scatter_dimension...  37.1 us
    dot_general x1, matrix products, expert_part(): return jnp.dot(activated, down_rows, preferred_element_type=jnp.float32)  17.6 us
    all_to_all x1, blocking collectives, body(): mine = lax.all_to_all(outgoing, 'exp', 0, 0, tiled=True)  10.8 us
    dot_general x1, matrix products, body(): projected = jnp.dot(settled, out_proj, preferred_element_type=jnp.float32)  9.5 us
  transfers between devices with their start and end apart: 4, of which 4 were waited for; matrix products, arithmetic and copies ran while one was open for 2% of the time, Pallas kernels for 0%

profile of v1, /device:TPU:0, one launch (start us, length us, event | category | flops | bytes accessed | tf_op | source)
XLA Modules:
  0.0 449.9 jit_solution(17354733472904034027)
XLA Ops:
  6.5 0.0 copy-start
  6.5 1.3 broadcast_multiply_fusion
  7.9 2.0 copy.27
  9.9 0.7 multiply_exponential_fusion
  10.6 2.2 convolution_convert_fusion.3
  12.8 0.0 all-gather.3.cloned.1.call-update
  12.8 0.0 reduce-scatter.3.cloned.1.call-start
  12.9 2.3 add_divide_fusion
  15.2 2.6 copy.25
  17.8 0.7 fusion.46
  18.5 0.8 fusion.45
  19.3 0.7 exponential_select_fusion
  20.0 48.5 %all-gather.3.cloned.1.call-done = bf16[256,128,128]{2,1,0:T(8,128)(2,1)} async-done(((bf16[8,128,128]{2,1,0:T(8,128)(2,1)}), bf16[256,128,128]{2,1,0:T(8,128)(2,1)}) %all-gather.3.cloned.1.call-update) | async-done | bytes 8388624 | tf_op jit(solution)/shard_map/all_gather | solution.py:11
  68.5 5.2 %fusion = f32[8,128,128]{2,1,0:T(8,128)S(1)} fusion(bf16[32,8,128,128]{3,2,1,0:T(8,128)(2,1)} %bitcast.96, f32[32,8]{1,0:T(8,128)S(1)} %exponential_select_fusion), kind=kLoop, calls=%fused_computation.1 | loop fusion | flops 12451840 | bytes 8913920 | tf_op jit(solution)/shard_map/reduce_sum | solution.py:18
  73.7 0.0 copy-start.8
  73.7 0.0 copy-done.4
  73.7 0.0 copy-done.5
  73.7 2.4 convolution_bitcast_fusion.2
  76.1 3.7 multiply_reduce_fusion.1
  79.8 1.8 multiply_convert_fusion.2
  81.5 9.5 %convolution_convert_fusion.1 = bf16[256,6144]{1,0:T(8,128)(2,1)} fusion(bf16[256,1024]{0,1:T(8,128)(2,1)S(1)} %bitcast.98, bf16[1024,6144]{1,0:T(8,128)(2,1)} %param.20), kind=kOutput, calls=%fused_computation.3 | convolution fusion | flops 3222798336 | bytes 16252928 | tf_op jit(solution)/shard_map/dot_general | solution.py:111
  91.1 0.0 reduce-scatter.3.cloned.1.call-update
  91.1 0.0 reduce-scatter.5.cloned.1.call-start
  91.1 0.6 copy-done.9
  91.7 0.1 constant_dynamic-slice_fusion
  91.8 0.1 iota_compare_fusion.3
  91.9 0.1 convolution_add_fusion
  92.0 37.1 %reduce-scatter.3.cloned.1.call-done = bf16[64,6144]{1,0:T(8,128)(2,1)} async-done(((bf16[256,6144]{1,0:T(8,128)(2,1)}), bf16[64,6144]{1,0:T(8,128)(2,1)}) %reduce-scatter.3.cloned.1.call-update) | async-done | bytes 786448 | tf_op jit(solution)/shard_map/reduce_scatter | solution.py:112
  129.1 1.7 multiply_reduce_fusion
  130.8 1.8 convolution_convert_fusion.2
  132.6 10.8 %all_to_all.15 = bf16[4,8,6144]{2,1,0:T(8,128)(2,1)S(1)} all-to-all(bf16[4,8,6144]{2,1,0:T(8,128)(2,1)S(1)} %convolution_convert_fusion.2), channel_id=1, replica_groups=mesh['ctx'=32,'exp'=4] {'exp'}, dimensions={0} | all-to-all | bytes 786432 | tf_op jit(solution)/shard_map/all_to_all | solution.py:123
  143.4 6.1 %stack.3 = bf16[32,32,6144]{2,1,0:T(8,128)(2,1)} broadcast(bf16[32,6144]{1,0:T(8,128)(2,1)S(1)} %bitcast.99), dimensions={1,2} | broadcast | bytes 12976128 | tf_op jit(solution)/shard_map/stack | solution.py:126
  149.5 148.4 %all_to_all.16 = bf16[32,32,6144]{2,1,0:T(8,128)(2,1)S(1)} all-to-all(bf16[32,32,6144]{2,1,0:T(8,128)(2,1)} %stack.3), channel_id=1, replica_groups=mesh['ctx'=32,'exp'=4] {'ctx'}, dimensions={0} | all-to-all | bytes 25165824 | tf_op jit(solution)/shard_map/all_to_all | solution.py:127
  298.0 4.5 copy-done.1
  302.4 0.0 copy-done.11
  302.4 5.0 %fusion.9 = f32[1024,288]{0,1:T(8,128)} fusion(bf16[1024,6144]{1,0:T(8,128)(2,1)S(1)} %bitcast.94, bf16[1,288,6144]{2,1,0:T(8,128)(2,1)S(1)} %copy-done.11), kind=kOutput, calls=%fused_computation.15 | convolution fusion | flops 3623878656 | bytes 17301504 | tf_op jit(solution)/shard_map/dot_general | solution.py:77
  307.4 17.6 %convolution_convert_fusion = bf16[1024,6144]{1,0:T(8,128)(2,1)} fusion(bf16[1,288,6144]{2,1,0:T(8,128)(2,1)S(1)} %copy-done, bf16[1024,6144]{1,0:T(8,128)(2,1)} %bitcast.95, bf16[1,288,6144]{2,1,0:T(8,128)(2,1)} %param.26, f32[1024,288]{0,1:T(8,128)} %fusion.9), kind=kOutput, calls=%fused_computation.2 | convolution fusion | flops 7255818240 | bytes 33423360 | tf_op jit(solution)/shard_map/dot_general | solution.py:84
  325.1 0.0 reduce-scatter.5.cloned.1.call-update
  325.1 0.7 copy-done.10
  325.8 0.1 constant_dynamic-slice_fusion.1
  325.8 102.0 %reduce-scatter.5.cloned.1.call-done = bf16[32,6144]{1,0:T(8,128)(2,1)} async-done(((bf16[1024,6144]{1,0:T(8,128)(2,1)}), bf16[32,6144]{1,0:T(8,128)(2,1)}) %reduce-scatter.5.cloned.1.call-update) | async-done | bytes 393232 | tf_op jit(solution)/shard_map/reduce_scatter | solution.py:129
  427.8 4.3 all-to-all-start.2
  432.1 0.5 slice_bitcast_fusion.3
  432.6 7.0 %all-to-all-done.2 = bf16[4,8,6144]{2,1,0:T(8,128)(2,1)} async-done(((bf16[4,8,6144]{2,1,0:T(8,128)(2,1)}), bf16[4,8,6144]{2,1,0:T(8,128)(2,1)}, u32[]{:S(2)}, u32[]{:S(2)}) %all-to-all-start.2) | async-done | bytes 393248 | tf_op jit(solution)/shard_map/all_to_all | solution.py:136
  439.6 1.5 fusion.4
  441.1 0.0 copy-done.2
  441.1 0.0 copy-done.3
  441.1 2.3 fusion.5
  (23 shorter events, 0.1 us)
Async XLA Ops:
  6.5 300.9 %copy-start = (bf16[1,288,6144]{2,1,0:T(8,128)(2,1)S(1)}, bf16[1,288,6144]{2,1,0:T(8,128)(2,1)}, u32[]{:S(2)}) copy-start(bf16[1,288,6144]{2,1,0:T(8,128)(2,1)} %param.27) | copy-start | bytes 10616836
  6.5 62.0 %all-gather.3.cloned.1.call-start = ((), (), s32[]{:S(2)}) async-start(), calls=%async_computation.7 | async-start | bytes 8650752 | tf_op jit(solution)/shard_map/all_gather | solution.py:11
  7.9 7.3 %copy-start.7 = (f32[8]{0:T(128)}, f32[8]{0:T(128)S(1)}, u32[]{:S(2)}) copy-start(f32[8]{0:T(128)S(1)} %get-tuple-element.6) | copy-start | bytes 100
  12.8 116.2 %reduce-scatter.3.cloned.1.call-start = ((), (), s32[]{:S(2)}) async-start(), calls=%async_computation.5 | async-start | bytes 3932160 | tf_op jit(solution)/shard_map/reduce_scatter | solution.py:112
  68.5 5.2 %copy-start.4 = (bf16[256,1024]{1,0:T(8,128)(2,1)S(1)}, bf16[256,1024]{1,0:T(8,128)(2,1)}, u32[]{:S(2)}) copy-start(bf16[256,1024]{1,0:T(8,128)(2,1)} %param.14) | copy-start | bytes 1572868
  68.5 5.2 %copy-start.5 = (f32[256,8]{0,1:T(8,128)S(1)}, f32[256,8]{0,1:T(8,128)}, u32[]{:S(2)}) copy-start(f32[256,8]{0,1:T(8,128)} %get-tuple-element.11) | copy-start | bytes 24580
  73.7 2.4 copy-start.8
  76.1 3.7 copy-start.6
  91.1 0.7 copy-start.9
  91.1 336.8 %reduce-scatter.5.cloned.1.call-start = ((), (), s32[]{:S(2)}) async-start(), calls=%async_computation.6 | async-start | bytes 12976128 | tf_op jit(solution)/shard_map/reduce_scatter | solution.py:129
  149.5 152.9 %copy-start.11 = (bf16[1,288,6144]{2,1,0:T(8,128)(2,1)S(1)}, bf16[1,288,6144]{2,1,0:T(8,128)(2,1)}, u32[]{:S(2)}) copy-start(bf16[1,288,6144]{2,1,0:T(8,128)(2,1)} %param.25) | copy-start | bytes 10616836
  298.0 4.5 copy-start.1
  325.1 0.7 copy-start.10
  427.8 11.8 %all-to-all-start.2 = ((bf16[4,8,6144]{2,1,0:T(8,128)(2,1)}), bf16[4,8,6144]{2,1,0:T(8,128)(2,1)}, u32[]{:S(2)}, u32[]{:S(2)}) async-start(bf16[4,8,6144]{2,1,0:T(8,128)(2,1)} %bitcast.102), calls=%async_computation.4 | async-start | bytes 786432 | tf_op jit(solution)/shard_map/all_to_all | solution.py:136
  439.6 1.5 copy-start.2
  439.6 1.5 copy-start.3
Sparse Core Ops, SparseCore 0:
  13.0 55.4 all-gather.2
  91.2 37.8 reduce-scatter.2
  325.2 102.5 reduce-scatter.4
